TPU v7x, 32 devices: a whole 2x2x4 slice. The times are simulated.
32 devices in a mesh: section: 4 (over y, x), rep: 8 (over z, core).
Axes of the slice: x: 2, y: 2, z: 4, core: 2. Of those that a mesh axis runs over, the one named last changes fastest.
Arguments:
- inputs: bfloat16 [6, 256, 6144], P(None, 'rep'), may hold values from -6 to 6
- cotangent: bfloat16 [6, 256, 6144], P(None, 'rep'), may hold values from -6 to 6
- in_weight: bfloat16 [4, 6144, 256], P('section', 'rep'), may hold values from -0.078125 to 0.078125
- out_weight: bfloat16 [4, 6144, 256], P('section', 'rep'), may hold values from -0.375 to 0.375
- norm_gain: float32 [4, 6144], P('section'), may hold values from 0.5 to 1.5
- lengths: int32 [8, 6], P('rep'), may hold values from 1 to 32, 144 in all within a row
Outputs:
- grad_in_weight: bfloat16 [4, 6144, 256], P('section', 'rep')
- grad_out_weight: bfloat16 [4, 6144, 256], P('section', 'rep')
- grad_gain: float32 [4, 6144], P('section')
- grad_inputs: bfloat16 [4, 6, 256, 6144], P('section', None, 'rep')
Inputs may be any that keep to these rules, and one draw needn't show every extreme that they name: `lengths`: each replica's 6 counts sum to 144 and the largest is 32.
All inputs are finite; a program needn't handle non-finite values.
Results may differ from a plain program's by a relative error of at most 0.025.
Values may be sent and summed in bfloat16 or wider, within the bound.
A program may use at most 64 MiB of HBM per device.

v0:
```python
import math
import jax
import jax.numpy as jnp
from jax import lax
from jax.sharding import PartitionSpec as P

norm_epsilon = 1e-05


def from_behind(block, axis, distance):
    devices = range(lax.axis_size(axis))
    route = [(i - distance, i) for i in devices if i - distance in devices]
    return lax.ppermute(block, axis, route)


def section_forward(hidden, norm_gain, in_weight, out_weight):
    widened = hidden.astype(jnp.float32)
    inverse = lax.rsqrt(jnp.mean(widened * widened, axis=-1, keepdims=True) + norm_epsilon)
    normed = (widened * inverse * norm_gain).astype(jnp.bfloat16)
    before = jnp.dot(normed, in_weight, preferred_element_type=jnp.float32)
    activated = jax.nn.silu(before).astype(jnp.bfloat16)
    mixed = lax.dot_general(
        activated, out_weight, (((1,), (1,)), ((), ())), preferred_element_type=jnp.float32
    )
    return ((widened + mixed).astype(jnp.bfloat16), normed, before, activated)


def section_backward(hidden, norm_gain, in_weight, out_weight, before, upstream):
    widened = hidden.astype(jnp.float32)
    inverse = lax.rsqrt(jnp.mean(widened * widened, axis=-1, keepdims=True) + norm_epsilon)
    grad_activated = jnp.dot(upstream, out_weight, preferred_element_type=jnp.float32)
    sigmoid_value = jax.nn.sigmoid(before)
    grad_before = (grad_activated * sigmoid_value * (1.0 + before * (1.0 - sigmoid_value))).astype(
        jnp.bfloat16
    )
    grad_normed = lax.dot_general(
        grad_before, in_weight, (((1,), (1,)), ((), ())), preferred_element_type=jnp.float32
    )
    grad_scaled = grad_normed * norm_gain
    projection = jnp.mean(grad_scaled * widened, axis=-1, keepdims=True)
    grad_hidden = (
        upstream.astype(jnp.float32)
        + inverse * grad_scaled
        - widened * (inverse * inverse * inverse) * projection
    )
    gain_terms = jnp.sum(grad_normed * widened * inverse, axis=0)
    return (grad_hidden.astype(jnp.bfloat16), grad_before, gain_terms)


def write_slot(holders, contents, slot):
    return tuple(
        (
            lax.dynamic_update_index_in_dim(holder, content, slot, 0)
            for holder, content in zip(holders, contents)
        )
    )


def body(inputs, cotangent, in_weight, out_weight, norm_gain, lengths):
    section_count = lax.axis_size("section")
    replicas = lax.axis_size("rep")
    position = lax.axis_index("section")
    micro_count, tok_rows, width = inputs.shape
    grad_scale = 1.0 / math.sqrt(micro_count * tok_rows * replicas)
    gain_row = norm_gain[0]
    full_in, full_out = (
        lax.all_gather(in_weight[0], "rep", axis=0, tiled=True),
        lax.all_gather(out_weight[0], "rep", axis=0, tiled=True),
    )
    rank_width = full_in.shape[1]
    tick_total = micro_count + section_count - 1
    blank = jnp.zeros((tok_rows, width), jnp.bfloat16)
    wide_zeros = jnp.zeros((micro_count, tok_rows, width), jnp.bfloat16)
    narrow_zeros = jnp.zeros((micro_count, tok_rows, rank_width), jnp.bfloat16)
    stores = (wide_zeros,)

    def forward_tick(moment, carried):
        received, holders = carried
        micro = moment - position
        active = (micro >= 0) & (micro < micro_count)
        slot = jnp.clip(micro, 0, micro_count - 1)
        fresh = lax.dynamic_index_in_dim(inputs, slot, 0, keepdims=False)
        entering = jnp.where(position == 0, fresh, received)

        def forward_run_section(holders):
            leaving, normed, before, activated = section_forward(
                entering, gain_row, full_in, full_out
            )
            contents = (entering,)
            return (leaving, write_slot(holders, contents, slot))

        def forward_skip_section(holders):
            return (blank, holders)

        leaving, holders = lax.cond(active, forward_run_section, forward_skip_section, holders)
        received = from_behind(leaving, "section", 1)
        return (received, holders)

    received, stores = lax.fori_loop(0, tick_total, forward_tick, (blank, stores))
    keep_rows = jnp.arange(tok_rows, dtype=jnp.int32)[None, :] < lengths[0][:, None]
    seeds = jnp.where(keep_rows[:, :, None], cotangent, jnp.zeros((), jnp.bfloat16))
    gain_start = jnp.zeros((width,), jnp.float32)
    buffers = (wide_zeros, narrow_zeros, wide_zeros, wide_zeros, narrow_zeros)

    def backward_tick(moment, carried):
        received, holders, gain_total = carried
        micro = moment - (section_count - 1 - position)
        active = (micro >= 0) & (micro < micro_count)
        slot = jnp.clip(micro, 0, micro_count - 1)
        seed_rows = lax.dynamic_index_in_dim(seeds, slot, 0, keepdims=False)
        entering = jnp.where(position == section_count - 1, seed_rows, received)

        def backward_run_section(operands):
            holders, gain_total = operands
            hidden_rows = lax.dynamic_index_in_dim(stores[0], slot, 0, keepdims=False)
            unused, normed, before, activated = section_forward(
                hidden_rows, gain_row, full_in, full_out
            )
            grad_hidden, grad_before, gain_terms = section_backward(
                hidden_rows, gain_row, full_in, full_out, before, entering
            )
            contents = (grad_hidden, grad_before, entering, normed, activated)
            return (grad_hidden, (write_slot(holders, contents, slot), gain_total + gain_terms))

        def backward_skip_section(operands):
            return (blank, operands)

        leaving, (holders, gain_total) = lax.cond(
            active, backward_run_section, backward_skip_section, (holders, gain_total)
        )
        received = from_behind(leaving, "section", -1)
        return (received, holders, gain_total)

    received, buffers, gain_total = lax.fori_loop(
        0, tick_total, backward_tick, (blank, buffers, gain_start)
    )
    normed_all = buffers[3]
    activated_all = buffers[4]
    flat_rows = micro_count * tok_rows
    normed_flat = normed_all.reshape(flat_rows, width)
    upstream_flat = buffers[2].reshape(flat_rows, width)
    before_flat = buffers[1].reshape(flat_rows, rank_width)
    activated_flat = activated_all.reshape(flat_rows, rank_width)
    left_term = lax.dot_general(
        normed_flat, before_flat, (((0,), (0,)), ((), ())), preferred_element_type=jnp.float32
    )
    right_term = lax.dot_general(
        upstream_flat, activated_flat, (((0,), (0,)), ((), ())), preferred_element_type=jnp.float32
    )
    summed = lax.psum_scatter(
        (jnp.concatenate((left_term, right_term), axis=1) * grad_scale).astype(jnp.bfloat16),
        "rep",
        scatter_dimension=0,
        tiled=True,
    ).astype(jnp.float32)
    grad_in_weight = summed[:, :rank_width].astype(jnp.bfloat16)[None]
    grad_out_weight = summed[:, rank_width:].astype(jnp.bfloat16)[None]
    grad_gain = lax.psum(gain_total * grad_scale, "rep")[None]
    grad_inputs = buffers[0][None]
    return (grad_in_weight, grad_out_weight, grad_gain, grad_inputs)


def solution(mesh):
    in_specs = (
        P(None, "rep", None),
        P(None, "rep", None),
        P("section", "rep", None),
        P("section", "rep", None),
        P("section", None),
        P("rep", None),
    )
    out_specs = (
        P("section", "rep", None),
        P("section", "rep", None),
        P("section", None),
        P("section", None, "rep", None),
    )
    return jax.shard_map(body, mesh=mesh, in_specs=in_specs, out_specs=out_specs, check_vma=False)
```

profile of v0, /device:TPU:0, one launch (start us, length us, event | category | flops | bytes accessed | tf_op | source)
XLA Modules:
  0.0 532.2 jit_solution(10388793744136409346)
XLA Ops:
  12.8 37.8 %all-gather.5.cloned.1.call-done = bf16[1,6144,256]{2,1,0:T(8,128)(2,1)} async-done(((bf16[1,768,256]{2,1,0:T(8,128)(2,1)}), bf16[1,6144,256]{2,1,0:T(8,128)(2,1)}) %all-gather.5.cloned.1.call-update) | async-done | bytes 3145744 | tf_op jit(solution)/shard_map/all_gather | solution.py:67
  50.6 38.8 %all-gather.7.cloned.1.call-done = bf16[1,6144,256]{2,1,0:T(8,128)(2,1)} async-done(((bf16[1,768,256]{2,1,0:T(8,128)(2,1)}), bf16[1,6144,256]{2,1,0:T(8,128)(2,1)}) %all-gather.7.cloned.1.call-update) | async-done | bytes 3145744 | tf_op jit(solution)/shard_map/all_gather | solution.py:68
  89.7 159.5 %while.46 = (s32[]{:T(128)}, bf16[32,6144]{1,0:T(8,128)(2,1)S(1)}, bf16[6,32,6144]{2,1,0:T(8,128)(2,1)S(1)}, s32[]{:T(128)}, pred[]{:T(512)}, /*index=5*/bf16[6,...) while((s32[]{:T(128)}, bf16[32,6144]{1,0:T(8,128)(2,1)S(1)}, ...), condition=%wide.region_4.5_spmd, body=%wide.region_0.4_spmd.sunk | while | flops 203530272 | bytes 12215116 | solution.py:99
  89.7 6.5 %conditional.4 = (bf16[32,6144]{1,0:T(8,128)(2,1)S(1)}, bf16[6,32,6144]{2,1,0:T(8,128)(2,1)S(1)}) conditional(s32[]{:T(128)} %convert_element_type.183, bf16[6,32,6144]{2,1,0:T(8,128)(2,1)S(1)} %get-tuple-element.1063, (pred[]{:T(512)}, s32[]{:T(128)}, bf16[6,32,6144]{2,1,0:T(8,128)(2,1)}, bf16[32,6144]{1,0:T(8,128)(2,1)S(1)}, ...), branch_computations={%region_1.1_spmd, %region_2.3_spmd} | conditional | flops 203530272 | bytes 9069101 | solution.py:95
  91.1 5.2 fusion
  98.3 9.3 %collective-permute-done = bf16[32,6144]{1,0:T(8,128)(2,1)S(1)} collective-permute-done((bf16[32,6144]{1,0:T(8,128)(2,1)}, bf16[32,6144]{1,0:T(8,128)(2,1)S(1)}, u32[]{:S(2)}, u32[]{:S(2)}) %collective-permute-start) | collective-permute-done | bytes 393248 | tf_op jit(solution)/shard_map/while/body/eval_jaxpr/ppermute | solution.py:13
  107.6 6.5 %conditional.4 = (bf16[32,6144]{1,0:T(8,128)(2,1)S(1)}, bf16[6,32,6144]{2,1,0:T(8,128)(2,1)S(1)}) conditional(s32[]{:T(128)} %convert_element_type.183, bf16[6,32,6144]{2,1,0:T(8,128)(2,1)S(1)} %get-tuple-element.1063, (pred[]{:T(512)}, s32[]{:T(128)}, bf16[6,32,6144]{2,1,0:T(8,128)(2,1)}, bf16[32,6144]{1,0:T(8,128)(2,1)S(1)}, ...), branch_computations={%region_1.1_spmd, %region_2.3_spmd} | conditional | flops 203530272 | bytes 9069101 | solution.py:95
  108.9 5.1 fusion
  114.8 4.3 collective-permute-start
  119.2 8.5 %collective-permute-done = bf16[32,6144]{1,0:T(8,128)(2,1)S(1)} collective-permute-done((bf16[32,6144]{1,0:T(8,128)(2,1)}, bf16[32,6144]{1,0:T(8,128)(2,1)S(1)}, u32[]{:S(2)}, u32[]{:S(2)}) %collective-permute-start) | collective-permute-done | bytes 393248 | tf_op jit(solution)/shard_map/while/body/eval_jaxpr/ppermute | solution.py:13
  127.6 6.5 %conditional.4 = (bf16[32,6144]{1,0:T(8,128)(2,1)S(1)}, bf16[6,32,6144]{2,1,0:T(8,128)(2,1)S(1)}) conditional(s32[]{:T(128)} %convert_element_type.183, bf16[6,32,6144]{2,1,0:T(8,128)(2,1)S(1)} %get-tuple-element.1063, (pred[]{:T(512)}, s32[]{:T(128)}, bf16[6,32,6144]{2,1,0:T(8,128)(2,1)}, bf16[32,6144]{1,0:T(8,128)(2,1)S(1)}, ...), branch_computations={%region_1.1_spmd, %region_2.3_spmd} | conditional | flops 203530272 | bytes 9069101 | solution.py:95
  128.9 5.2 fusion
  139.2 7.6 %collective-permute-done = bf16[32,6144]{1,0:T(8,128)(2,1)S(1)} collective-permute-done((bf16[32,6144]{1,0:T(8,128)(2,1)}, bf16[32,6144]{1,0:T(8,128)(2,1)S(1)}, u32[]{:S(2)}, u32[]{:S(2)}) %collective-permute-start) | collective-permute-done | bytes 393248 | tf_op jit(solution)/shard_map/while/body/eval_jaxpr/ppermute | solution.py:13
  146.8 6.5 %conditional.4 = (bf16[32,6144]{1,0:T(8,128)(2,1)S(1)}, bf16[6,32,6144]{2,1,0:T(8,128)(2,1)S(1)}) conditional(s32[]{:T(128)} %convert_element_type.183, bf16[6,32,6144]{2,1,0:T(8,128)(2,1)S(1)} %get-tuple-element.1063, (pred[]{:T(512)}, s32[]{:T(128)}, bf16[6,32,6144]{2,1,0:T(8,128)(2,1)}, bf16[32,6144]{1,0:T(8,128)(2,1)S(1)}, ...), branch_computations={%region_1.1_spmd, %region_2.3_spmd} | conditional | flops 203530272 | bytes 9069101 | solution.py:95
  148.1 5.2 fusion
  158.3 6.8 %collective-permute-done = bf16[32,6144]{1,0:T(8,128)(2,1)S(1)} collective-permute-done((bf16[32,6144]{1,0:T(8,128)(2,1)}, bf16[32,6144]{1,0:T(8,128)(2,1)S(1)}, u32[]{:S(2)}, u32[]{:S(2)}) %collective-permute-start) | collective-permute-done | bytes 393248 | tf_op jit(solution)/shard_map/while/body/eval_jaxpr/ppermute | solution.py:13
  165.1 6.5 %conditional.4 = (bf16[32,6144]{1,0:T(8,128)(2,1)S(1)}, bf16[6,32,6144]{2,1,0:T(8,128)(2,1)S(1)}) conditional(s32[]{:T(128)} %convert_element_type.183, bf16[6,32,6144]{2,1,0:T(8,128)(2,1)S(1)} %get-tuple-element.1063, (pred[]{:T(512)}, s32[]{:T(128)}, bf16[6,32,6144]{2,1,0:T(8,128)(2,1)}, bf16[32,6144]{1,0:T(8,128)(2,1)S(1)}, ...), branch_computations={%region_1.1_spmd, %region_2.3_spmd} | conditional | flops 203530272 | bytes 9069101 | solution.py:95
  166.4 5.2 fusion
  172.3 4.5 collective-permute-start
  176.9 6.2 %collective-permute-done = bf16[32,6144]{1,0:T(8,128)(2,1)S(1)} collective-permute-done((bf16[32,6144]{1,0:T(8,128)(2,1)}, bf16[32,6144]{1,0:T(8,128)(2,1)S(1)}, u32[]{:S(2)}, u32[]{:S(2)}) %collective-permute-start) | collective-permute-done | bytes 393248 | tf_op jit(solution)/shard_map/while/body/eval_jaxpr/ppermute | solution.py:13
  183.0 6.5 %conditional.4 = (bf16[32,6144]{1,0:T(8,128)(2,1)S(1)}, bf16[6,32,6144]{2,1,0:T(8,128)(2,1)S(1)}) conditional(s32[]{:T(128)} %convert_element_type.183, bf16[6,32,6144]{2,1,0:T(8,128)(2,1)S(1)} %get-tuple-element.1063, (pred[]{:T(512)}, s32[]{:T(128)}, bf16[6,32,6144]{2,1,0:T(8,128)(2,1)}, bf16[32,6144]{1,0:T(8,128)(2,1)S(1)}, ...), branch_computations={%region_1.1_spmd, %region_2.3_spmd} | conditional | flops 203530272 | bytes 9069101 | solution.py:95
  184.3 5.2 fusion
  190.3 5.2 collective-permute-start
  195.5 5.6 %collective-permute-done = bf16[32,6144]{1,0:T(8,128)(2,1)S(1)} collective-permute-done((bf16[32,6144]{1,0:T(8,128)(2,1)}, bf16[32,6144]{1,0:T(8,128)(2,1)S(1)}, u32[]{:S(2)}, u32[]{:S(2)}) %collective-permute-start) | collective-permute-done | bytes 393248 | tf_op jit(solution)/shard_map/while/body/eval_jaxpr/ppermute | solution.py:13
  201.8 11.7 %collective-permute-start = (bf16[32,6144]{1,0:T(8,128)(2,1)}, bf16[32,6144]{1,0:T(8,128)(2,1)S(1)}, u32[]{:S(2)}, u32[]{:S(2)}) collective-permute-start(bf16[32,6144]{1,0:T(8,128)(2,1)} %copy-done.5), channel_id=1, source_target_pairs={{0,8},{8,16},{16,24},{1,9},{9,17},{17,25},{2,10},{10,18},{18,26},{... | collective-permute-start | bytes 1179656 | tf_op jit(solution)/shard_map/while/body/eval_jaxpr/ppermute | solution.py:13
  213.5 5.6 %collective-permute-done = bf16[32,6144]{1,0:T(8,128)(2,1)S(1)} collective-permute-done((bf16[32,6144]{1,0:T(8,128)(2,1)}, bf16[32,6144]{1,0:T(8,128)(2,1)S(1)}, u32[]{:S(2)}, u32[]{:S(2)}) %collective-permute-start) | collective-permute-done | bytes 393248 | tf_op jit(solution)/shard_map/while/body/eval_jaxpr/ppermute | solution.py:13
  219.8 5.2 collective-permute-start
  225.0 5.6 %collective-permute-done = bf16[32,6144]{1,0:T(8,128)(2,1)S(1)} collective-permute-done((bf16[32,6144]{1,0:T(8,128)(2,1)}, bf16[32,6144]{1,0:T(8,128)(2,1)S(1)}, u32[]{:S(2)}, u32[]{:S(2)}) %collective-permute-start) | collective-permute-done | bytes 393248 | tf_op jit(solution)/shard_map/while/body/eval_jaxpr/ppermute | solution.py:13
  231.4 12.2 %collective-permute-start = (bf16[32,6144]{1,0:T(8,128)(2,1)}, bf16[32,6144]{1,0:T(8,128)(2,1)S(1)}, u32[]{:S(2)}, u32[]{:S(2)}) collective-permute-start(bf16[32,6144]{1,0:T(8,128)(2,1)} %copy-done.5), channel_id=1, source_target_pairs={{0,8},{8,16},{16,24},{1,9},{9,17},{17,25},{2,10},{10,18},{18,26},{... | collective-permute-start | bytes 1179656 | tf_op jit(solution)/shard_map/while/body/eval_jaxpr/ppermute | solution.py:13
  243.6 5.6 %collective-permute-done = bf16[32,6144]{1,0:T(8,128)(2,1)S(1)} collective-permute-done((bf16[32,6144]{1,0:T(8,128)(2,1)}, bf16[32,6144]{1,0:T(8,128)(2,1)S(1)}, u32[]{:S(2)}, u32[]{:S(2)}) %collective-permute-start) | collective-permute-done | bytes 393248 | tf_op jit(solution)/shard_map/while/body/eval_jaxpr/ppermute | solution.py:13
  255.9 191.4 %while.47 = (s32[]{:T(128)}, bf16[32,6144]{1,0:T(8,128)(2,1)}, bf16[6,32,6144]{2,1,0:T(8,128)(2,1)}, bf16[6,32,256]{2,1,0:T(8,128)(2,1)S(1)}, bf16[6,32,6144]{2,...) while((s32[]{:T(128)}, bf16[32,6144]{1,0:T(8,128)(2,1)}, ...), condition=%wide.region_11.12_spmd, body=%wide.region_5.11_spmd.sunk | while | flops 307413088 | bytes 30610964 | solution.py:134
  257.9 9.9 %collective-permute-done.1 = bf16[32,6144]{1,0:T(8,128)(2,1)} collective-permute-done((bf16[32,6144]{1,0:T(8,128)(2,1)}, bf16[32,6144]{1,0:T(8,128)(2,1)}, u32[]{:S(2)}, u32[]{:S(2)}) %collective-permute-start.1) | collective-permute-done | bytes 393248 | tf_op jit(solution)/shard_map/while/body/eval_jaxpr/ppermute | solution.py:13
  269.9 11.7 %collective-permute-done.1 = bf16[32,6144]{1,0:T(8,128)(2,1)} collective-permute-done((bf16[32,6144]{1,0:T(8,128)(2,1)}, bf16[32,6144]{1,0:T(8,128)(2,1)}, u32[]{:S(2)}, u32[]{:S(2)}) %collective-permute-start.1) | collective-permute-done | bytes 393248 | tf_op jit(solution)/shard_map/while/body/eval_jaxpr/ppermute | solution.py:13
  283.7 36.6 %collective-permute-done.1 = bf16[32,6144]{1,0:T(8,128)(2,1)} collective-permute-done((bf16[32,6144]{1,0:T(8,128)(2,1)}, bf16[32,6144]{1,0:T(8,128)(2,1)}, u32[]{:S(2)}, u32[]{:S(2)}) %collective-permute-start.1) | collective-permute-done | bytes 393248 | tf_op jit(solution)/shard_map/while/body/eval_jaxpr/ppermute | solution.py:13
  320.3 10.2 %conditional.5 = (bf16[32,6144]{1,0:T(8,128)(2,1)}, bf16[6,32,6144]{2,1,0:T(8,128)(2,1)}, bf16[6,32,256]{2,1,0:T(8,128)(2,1)S(1)}, bf16[6,32,6144]{2,1,0:T(8,128...) conditional(s32[]{:T(128)} %convert_element_type.184, ...), branch_computations={%region_6.6_spmd, %region_7.10_spmd} | conditional | flops 307413088 | bytes 29037696 | solution.py:128
  331.8 9.6 %collective-permute-done.1 = bf16[32,6144]{1,0:T(8,128)(2,1)} collective-permute-done((bf16[32,6144]{1,0:T(8,128)(2,1)}, bf16[32,6144]{1,0:T(8,128)(2,1)}, u32[]{:S(2)}, u32[]{:S(2)}) %collective-permute-start.1) | collective-permute-done | bytes 393248 | tf_op jit(solution)/shard_map/while/body/eval_jaxpr/ppermute | solution.py:13
  341.4 10.2 %conditional.5 = (bf16[32,6144]{1,0:T(8,128)(2,1)}, bf16[6,32,6144]{2,1,0:T(8,128)(2,1)}, bf16[6,32,256]{2,1,0:T(8,128)(2,1)S(1)}, bf16[6,32,6144]{2,1,0:T(8,128...) conditional(s32[]{:T(128)} %convert_element_type.184, ...), branch_computations={%region_6.6_spmd, %region_7.10_spmd} | conditional | flops 307413088 | bytes 29037696 | solution.py:128
  352.9 9.6 %collective-permute-done.1 = bf16[32,6144]{1,0:T(8,128)(2,1)} collective-permute-done((bf16[32,6144]{1,0:T(8,128)(2,1)}, bf16[32,6144]{1,0:T(8,128)(2,1)}, u32[]{:S(2)}, u32[]{:S(2)}) %collective-permute-start.1) | collective-permute-done | bytes 393248 | tf_op jit(solution)/shard_map/while/body/eval_jaxpr/ppermute | solution.py:13
  362.5 10.2 %conditional.5 = (bf16[32,6144]{1,0:T(8,128)(2,1)}, bf16[6,32,6144]{2,1,0:T(8,128)(2,1)}, bf16[6,32,256]{2,1,0:T(8,128)(2,1)S(1)}, bf16[6,32,6144]{2,1,0:T(8,128...) conditional(s32[]{:T(128)} %convert_element_type.184, ...), branch_computations={%region_6.6_spmd, %region_7.10_spmd} | conditional | flops 307413088 | bytes 29037696 | solution.py:128
  374.0 9.6 %collective-permute-done.1 = bf16[32,6144]{1,0:T(8,128)(2,1)} collective-permute-done((bf16[32,6144]{1,0:T(8,128)(2,1)}, bf16[32,6144]{1,0:T(8,128)(2,1)}, u32[]{:S(2)}, u32[]{:S(2)}) %collective-permute-start.1) | collective-permute-done | bytes 393248 | tf_op jit(solution)/shard_map/while/body/eval_jaxpr/ppermute | solution.py:13
  383.6 10.3 %conditional.5 = (bf16[32,6144]{1,0:T(8,128)(2,1)}, bf16[6,32,6144]{2,1,0:T(8,128)(2,1)}, bf16[6,32,256]{2,1,0:T(8,128)(2,1)S(1)}, bf16[6,32,6144]{2,1,0:T(8,128...) conditional(s32[]{:T(128)} %convert_element_type.184, ...), branch_computations={%region_6.6_spmd, %region_7.10_spmd} | conditional | flops 307413088 | bytes 29037696 | solution.py:128
  395.2 9.6 %collective-permute-done.1 = bf16[32,6144]{1,0:T(8,128)(2,1)} collective-permute-done((bf16[32,6144]{1,0:T(8,128)(2,1)}, bf16[32,6144]{1,0:T(8,128)(2,1)}, u32[]{:S(2)}, u32[]{:S(2)}) %collective-permute-start.1) | collective-permute-done | bytes 393248 | tf_op jit(solution)/shard_map/while/body/eval_jaxpr/ppermute | solution.py:13
  404.8 10.3 %conditional.5 = (bf16[32,6144]{1,0:T(8,128)(2,1)}, bf16[6,32,6144]{2,1,0:T(8,128)(2,1)}, bf16[6,32,256]{2,1,0:T(8,128)(2,1)S(1)}, bf16[6,32,6144]{2,1,0:T(8,128...) conditional(s32[]{:T(128)} %convert_element_type.184, ...), branch_computations={%region_6.6_spmd, %region_7.10_spmd} | conditional | flops 307413088 | bytes 29037696 | solution.py:128
  416.3 10.7 %collective-permute-done.1 = bf16[32,6144]{1,0:T(8,128)(2,1)} collective-permute-done((bf16[32,6144]{1,0:T(8,128)(2,1)}, bf16[32,6144]{1,0:T(8,128)(2,1)}, u32[]{:S(2)}, u32[]{:S(2)}) %collective-permute-start.1) | collective-permute-done | bytes 393248 | tf_op jit(solution)/shard_map/while/body/eval_jaxpr/ppermute | solution.py:13
  427.0 10.3 %conditional.5 = (bf16[32,6144]{1,0:T(8,128)(2,1)}, bf16[6,32,6144]{2,1,0:T(8,128)(2,1)}, bf16[6,32,256]{2,1,0:T(8,128)(2,1)S(1)}, bf16[6,32,6144]{2,1,0:T(8,128...) conditional(s32[]{:T(128)} %convert_element_type.184, ...), branch_computations={%region_6.6_spmd, %region_7.10_spmd} | conditional | flops 307413088 | bytes 29037696 | solution.py:128
  438.6 8.7 %collective-permute-done.1 = bf16[32,6144]{1,0:T(8,128)(2,1)} collective-permute-done((bf16[32,6144]{1,0:T(8,128)(2,1)}, bf16[32,6144]{1,0:T(8,128)(2,1)}, u32[]{:S(2)}, u32[]{:S(2)}) %collective-permute-start.1) | collective-permute-done | bytes 393248 | tf_op jit(solution)/shard_map/while/body/eval_jaxpr/ppermute | solution.py:13
  455.0 27.8 %psum.7 = f32[1,6144]{1,0:T(1,128)} all-reduce(f32[1,6144]{1,0:T(1,128)S(1)} %bitcast.83), channel_id=1, replica_groups=mesh['section'=4,'rep'=8] {'rep'}, use_global_device_ids=true, to_apply=%region_13.14 | all-reduce | flops 6144 | bytes 49152 | tf_op jit(solution)/shard_map/psum | solution.py:158
  482.9 39.8 %reduce-scatter.2.cloned.1.call-done = bf16[768,512]{0,1:T(8,128)(2,1)} async-done(((bf16[6144,512]{0,1:T(8,128)(2,1)}), bf16[768,512]{0,1:T(8,128)(2,1)}) %reduce-scatter.2.cloned.1.call-update) | async-done | bytes 786448 | tf_op jit(solution)/shard_map/reduce_scatter | solution.py:150
  (158 shorter events, 125.4 us)
Async XLA Ops:
  7.2 43.4 %all-gather.5.cloned.1.call-start = ((), (), s32[]{:S(2)}) async-start(), calls=%async_computation.2 | async-start | bytes 3538944 | tf_op jit(solution)/shard_map/all_gather | solution.py:67
  7.9 81.5 %all-gather.7.cloned.1.call-start = ((), (), s32[]{:S(2)}) async-start(), calls=%async_computation.3 | async-start | bytes 3538944 | tf_op jit(solution)/shard_map/all_gather | solution.py:68
  8.6 514.0 %reduce-scatter.2.cloned.1.call-start = ((), (), s32[]{:S(2)}) async-start(), calls=%async_computation.1 | async-start | bytes 7077888 | tf_op jit(solution)/shard_map/reduce_scatter | solution.py:150
  12.8 76.9 %copy-start.3 = (f32[1,6144]{1,0:T(1,128)S(1)}, f32[1,6144]{1,0:T(1,128)}, u32[]{:S(2)}) copy-start(f32[1,6144]{1,0:T(1,128)} %param.18) | copy-start | bytes 73732
  96.2 0.8 copy-start.5
  97.0 10.6 %collective-permute-start = (bf16[32,6144]{1,0:T(8,128)(2,1)}, bf16[32,6144]{1,0:T(8,128)(2,1)S(1)}, u32[]{:S(2)}, u32[]{:S(2)}) collective-permute-start(bf16[32,6144]{1,0:T(8,128)(2,1)} %copy-done.5), channel_id=1, source_target_pairs={{0,8},{8,16},{16,24},{1,9},{9,17},{17,25},{2,10},{10,18},{18,26},{... | collective-permute-start | bytes 1179656 | tf_op jit(solution)/shard_map/while/body/eval_jaxpr/ppermute | solution.py:13
  114.1 0.8 copy-start.5
  114.8 12.8 %collective-permute-start = (bf16[32,6144]{1,0:T(8,128)(2,1)}, bf16[32,6144]{1,0:T(8,128)(2,1)S(1)}, u32[]{:S(2)}, u32[]{:S(2)}) collective-permute-start(bf16[32,6144]{1,0:T(8,128)(2,1)} %copy-done.5), channel_id=1, source_target_pairs={{0,8},{8,16},{16,24},{1,9},{9,17},{17,25},{2,10},{10,18},{18,26},{... | collective-permute-start | bytes 1179656 | tf_op jit(solution)/shard_map/while/body/eval_jaxpr/ppermute | solution.py:13
  134.1 0.8 copy-start.5
  134.9 11.9 %collective-permute-start = (bf16[32,6144]{1,0:T(8,128)(2,1)}, bf16[32,6144]{1,0:T(8,128)(2,1)S(1)}, u32[]{:S(2)}, u32[]{:S(2)}) collective-permute-start(bf16[32,6144]{1,0:T(8,128)(2,1)} %copy-done.5), channel_id=1, source_target_pairs={{0,8},{8,16},{16,24},{1,9},{9,17},{17,25},{2,10},{10,18},{18,26},{... | collective-permute-start | bytes 1179656 | tf_op jit(solution)/shard_map/while/body/eval_jaxpr/ppermute | solution.py:13
  153.2 0.8 copy-start.5
  154.0 11.1 %collective-permute-start = (bf16[32,6144]{1,0:T(8,128)(2,1)}, bf16[32,6144]{1,0:T(8,128)(2,1)S(1)}, u32[]{:S(2)}, u32[]{:S(2)}) collective-permute-start(bf16[32,6144]{1,0:T(8,128)(2,1)} %copy-done.5), channel_id=1, source_target_pairs={{0,8},{8,16},{16,24},{1,9},{9,17},{17,25},{2,10},{10,18},{18,26},{... | collective-permute-start | bytes 1179656 | tf_op jit(solution)/shard_map/while/body/eval_jaxpr/ppermute | solution.py:13
  171.5 0.8 copy-start.5
  172.3 10.7 %collective-permute-start = (bf16[32,6144]{1,0:T(8,128)(2,1)}, bf16[32,6144]{1,0:T(8,128)(2,1)S(1)}, u32[]{:S(2)}, u32[]{:S(2)}) collective-permute-start(bf16[32,6144]{1,0:T(8,128)(2,1)} %copy-done.5), channel_id=1, source_target_pairs={{0,8},{8,16},{16,24},{1,9},{9,17},{17,25},{2,10},{10,18},{18,26},{... | collective-permute-start | bytes 1179656 | tf_op jit(solution)/shard_map/while/body/eval_jaxpr/ppermute | solution.py:13
  189.5 0.8 copy-start.5
  190.3 10.8 %collective-permute-start = (bf16[32,6144]{1,0:T(8,128)(2,1)}, bf16[32,6144]{1,0:T(8,128)(2,1)S(1)}, u32[]{:S(2)}, u32[]{:S(2)}) collective-permute-start(bf16[32,6144]{1,0:T(8,128)(2,1)} %copy-done.5), channel_id=1, source_target_pairs={{0,8},{8,16},{16,24},{1,9},{9,17},{17,25},{2,10},{10,18},{18,26},{... | collective-permute-start | bytes 1179656 | tf_op jit(solution)/shard_map/while/body/eval_jaxpr/ppermute | solution.py:13
  201.1 0.7 copy-start.5
  201.8 17.2 %collective-permute-start = (bf16[32,6144]{1,0:T(8,128)(2,1)}, bf16[32,6144]{1,0:T(8,128)(2,1)S(1)}, u32[]{:S(2)}, u32[]{:S(2)}) collective-permute-start(bf16[32,6144]{1,0:T(8,128)(2,1)} %copy-done.5), channel_id=1, source_target_pairs={{0,8},{8,16},{16,24},{1,9},{9,17},{17,25},{2,10},{10,18},{18,26},{... | collective-permute-start | bytes 1179656 | tf_op jit(solution)/shard_map/while/body/eval_jaxpr/ppermute | solution.py:13
  219.1 0.7 copy-start.5
  219.8 10.8 %collective-permute-start = (bf16[32,6144]{1,0:T(8,128)(2,1)}, bf16[32,6144]{1,0:T(8,128)(2,1)S(1)}, u32[]{:S(2)}, u32[]{:S(2)}) collective-permute-start(bf16[32,6144]{1,0:T(8,128)(2,1)} %copy-done.5), channel_id=1, source_target_pairs={{0,8},{8,16},{16,24},{1,9},{9,17},{17,25},{2,10},{10,18},{18,26},{... | collective-permute-start | bytes 1179656 | tf_op jit(solution)/shard_map/while/body/eval_jaxpr/ppermute | solution.py:13
  230.6 0.7 copy-start.5
  231.4 17.8 %collective-permute-start = (bf16[32,6144]{1,0:T(8,128)(2,1)}, bf16[32,6144]{1,0:T(8,128)(2,1)S(1)}, u32[]{:S(2)}, u32[]{:S(2)}) collective-permute-start(bf16[32,6144]{1,0:T(8,128)(2,1)} %copy-done.5), channel_id=1, source_target_pairs={{0,8},{8,16},{16,24},{1,9},{9,17},{17,25},{2,10},{10,18},{18,26},{... | collective-permute-start | bytes 1179656 | tf_op jit(solution)/shard_map/while/body/eval_jaxpr/ppermute | solution.py:13
  249.2 1.6 copy-start.2
  252.4 3.4 copy-start
  256.6 11.2 %collective-permute-start.1 = (bf16[32,6144]{1,0:T(8,128)(2,1)}, bf16[32,6144]{1,0:T(8,128)(2,1)}, u32[]{:S(2)}, u32[]{:S(2)}) collective-permute-start(bf16[32,6144]{1,0:T(8,128)(2,1)} %get-tuple-element.1024), channel_id=1, source_target_pairs={{8,0},{16,8},{24,16},{9,1},{17,9},{25,17},{10,2},{18,10},{26,18},{... | collective-permute-start | bytes 1179656 | tf_op jit(solution)/shard_map/while/body/eval_jaxpr/ppermute | solution.py:13
  268.6 13.0 %collective-permute-start.1 = (bf16[32,6144]{1,0:T(8,128)(2,1)}, bf16[32,6144]{1,0:T(8,128)(2,1)}, u32[]{:S(2)}, u32[]{:S(2)}) collective-permute-start(bf16[32,6144]{1,0:T(8,128)(2,1)} %get-tuple-element.1024), channel_id=1, source_target_pairs={{8,0},{16,8},{24,16},{9,1},{17,9},{25,17},{10,2},{18,10},{26,18},{... | collective-permute-start | bytes 1179656 | tf_op jit(solution)/shard_map/while/body/eval_jaxpr/ppermute | solution.py:13
  282.4 37.9 %collective-permute-start.1 = (bf16[32,6144]{1,0:T(8,128)(2,1)}, bf16[32,6144]{1,0:T(8,128)(2,1)}, u32[]{:S(2)}, u32[]{:S(2)}) collective-permute-start(bf16[32,6144]{1,0:T(8,128)(2,1)} %get-tuple-element.1024), channel_id=1, source_target_pairs={{8,0},{16,8},{24,16},{9,1},{17,9},{25,17},{10,2},{18,10},{26,18},{... | collective-permute-start | bytes 1179656 | tf_op jit(solution)/shard_map/while/body/eval_jaxpr/ppermute | solution.py:13
  321.5 3.9 copy-start.1
  330.5 10.9 %collective-permute-start.1 = (bf16[32,6144]{1,0:T(8,128)(2,1)}, bf16[32,6144]{1,0:T(8,128)(2,1)}, u32[]{:S(2)}, u32[]{:S(2)}) collective-permute-start(bf16[32,6144]{1,0:T(8,128)(2,1)} %get-tuple-element.1024), channel_id=1, source_target_pairs={{8,0},{16,8},{24,16},{9,1},{17,9},{25,17},{10,2},{18,10},{26,18},{... | collective-permute-start | bytes 1179656 | tf_op jit(solution)/shard_map/while/body/eval_jaxpr/ppermute | solution.py:13
  342.6 3.9 copy-start.1
  351.7 10.8 %collective-permute-start.1 = (bf16[32,6144]{1,0:T(8,128)(2,1)}, bf16[32,6144]{1,0:T(8,128)(2,1)}, u32[]{:S(2)}, u32[]{:S(2)}) collective-permute-start(bf16[32,6144]{1,0:T(8,128)(2,1)} %get-tuple-element.1024), channel_id=1, source_target_pairs={{8,0},{16,8},{24,16},{9,1},{17,9},{25,17},{10,2},{18,10},{26,18},{... | collective-permute-start | bytes 1179656 | tf_op jit(solution)/shard_map/while/body/eval_jaxpr/ppermute | solution.py:13
  363.7 3.9 copy-start.1
  372.7 10.9 %collective-permute-start.1 = (bf16[32,6144]{1,0:T(8,128)(2,1)}, bf16[32,6144]{1,0:T(8,128)(2,1)}, u32[]{:S(2)}, u32[]{:S(2)}) collective-permute-start(bf16[32,6144]{1,0:T(8,128)(2,1)} %get-tuple-element.1024), channel_id=1, source_target_pairs={{8,0},{16,8},{24,16},{9,1},{17,9},{25,17},{10,2},{18,10},{26,18},{... | collective-permute-start | bytes 1179656 | tf_op jit(solution)/shard_map/while/body/eval_jaxpr/ppermute | solution.py:13
  384.8 3.9 copy-start.1
  393.9 10.9 %collective-permute-start.1 = (bf16[32,6144]{1,0:T(8,128)(2,1)}, bf16[32,6144]{1,0:T(8,128)(2,1)}, u32[]{:S(2)}, u32[]{:S(2)}) collective-permute-start(bf16[32,6144]{1,0:T(8,128)(2,1)} %get-tuple-element.1024), channel_id=1, source_target_pairs={{8,0},{16,8},{24,16},{9,1},{17,9},{25,17},{10,2},{18,10},{26,18},{... | collective-permute-start | bytes 1179656 | tf_op jit(solution)/shard_map/while/body/eval_jaxpr/ppermute | solution.py:13
  406.0 3.9 copy-start.1
  415.1 12.0 %collective-permute-start.1 = (bf16[32,6144]{1,0:T(8,128)(2,1)}, bf16[32,6144]{1,0:T(8,128)(2,1)}, u32[]{:S(2)}, u32[]{:S(2)}) collective-permute-start(bf16[32,6144]{1,0:T(8,128)(2,1)} %get-tuple-element.1024), channel_id=1, source_target_pairs={{8,0},{16,8},{24,16},{9,1},{17,9},{25,17},{10,2},{18,10},{26,18},{... | collective-permute-start | bytes 1179656 | tf_op jit(solution)/shard_map/while/body/eval_jaxpr/ppermute | solution.py:13
  428.2 3.9 copy-start.1
  437.3 10.0 %collective-permute-start.1 = (bf16[32,6144]{1,0:T(8,128)(2,1)}, bf16[32,6144]{1,0:T(8,128)(2,1)}, u32[]{:S(2)}, u32[]{:S(2)}) collective-permute-start(bf16[32,6144]{1,0:T(8,128)(2,1)} %get-tuple-element.1024), channel_id=1, source_target_pairs={{8,0},{16,8},{24,16},{9,1},{17,9},{25,17},{10,2},{18,10},{26,18},{... | collective-permute-start | bytes 1179656 | tf_op jit(solution)/shard_map/while/body/eval_jaxpr/ppermute | solution.py:13
  447.3 2.8 copy-start.4
Sparse Core Ops, SparseCore 0:
  9.6 40.9 all-gather.4
  52.2 37.1 all-gather.6
  455.2 67.4 reduce-scatter.1
where the time goes:
time: 534 us; the launch traced here: 532 us
  waiting for transfers between devices  294 us (55%)
  starting transfers between devices  64.6 us (12%)
  matrix products  63 us (12%)
  other arithmetic  48.9 us (9%)
  blocking collectives  27.8 us (5%)
  local copies, waits for them, and re-layouts  19.1 us (4%)
  between operations  13.8 us (3%)
    ppermute x18, waiting for transfers between devices, from_behind(): return lax.ppermute(block, axis, route)  177 us
    ppermute x18, starting transfers between devices, from_behind(): return lax.ppermute(block, axis, route)  64.5 us
    reduce_scatter x1, waiting for transfers between devices, body(): lax.psum_scatter((jnp.concatenate((left_term, right_term), axis=1) * grad...  39.8 us
    all_gather x1, waiting for transfers between devices, body(): lax.all_gather(out_weight[0], 'rep', axis=0, tiled=True)  38.8 us
    all_gather x1, waiting for transfers between devices, body(): lax.all_gather(in_weight[0], 'rep', axis=0, tiled=True)  37.8 us
    dynamic_update_slice x18, other arithmetic, write_slot(): lax.dynamic_update_index_in_dim(holder, content, slot, 0)  32.5 us
    dot_general x6, matrix products, section_forward(): lax.dot_general(activated, out_weight, (((1,), (1,)), ((), ())), preferre...  30.9 us
    psum x1, blocking collectives, body(): grad_gain = lax.psum(gain_total * grad_scale, 'rep')[None]  27.8 us
  transfers between devices with their start and end apart: 21, of which 21 were waited for; matrix products, arithmetic and copies ran while one was open for 1% of the time, Pallas kernels for 0%

commit v1 on v0

--- a/solution.py
+++ b/solution.py
@@ -5,6 +5,28 @@
 from jax.sharding import PartitionSpec as P
 
 norm_epsilon = 1e-05
+
+
+def joined_along(blocks, dim):
+    blocks = jnp.moveaxis(blocks, 0, dim)
+    dims = blocks.shape
+    return blocks.reshape(*dims[:dim], dims[dim] * dims[dim + 1], *dims[dim + 2 :])
+
+
+def gather_around(x, axis, dim):
+    count = lax.axis_size(axis)
+    pairs = [(i, (i + 1) % count) for i in range(count)]
+    back = [(b, a) for a, b in pairs]
+    lower, upper = ([], [])
+    for step in range(count - 1):
+        if step % 2 == 0:
+            lower.append(lax.ppermute(lower[-1] if lower else x, axis, pairs))
+        else:
+            upper.append(lax.ppermute(upper[-1] if upper else x, axis, back))
+    blocks = jnp.stack([*lower[::-1], x, *upper])
+    shift = lax.axis_index(axis) - len(lower)
+    blocks = blocks[(jnp.arange(count) - shift) % count]
+    return joined_along(blocks, dim)
 
 
 def from_behind(block, axis, distance):
@@ -65,7 +87,7 @@
     gain_row = norm_gain[0]
     full_in, full_out = (
         lax.all_gather(in_weight[0], "rep", axis=0, tiled=True),
-        lax.all_gather(out_weight[0], "rep", axis=0, tiled=True),
+        gather_around(out_weight[0], "rep", 0),
     )
     rank_width = full_in.shape[1]
     tick_total = micro_count + section_count - 1

time: 534 us -> 552 us (1.034)
  waiting for transfers between devices: 294 us -> 261 us
  local copies, waits for them, and re-layouts: 19.1 us -> 33.9 us
  blocking collectives: 27.8 us -> 41.5 us
  starting transfers between devices: 64.6 us -> 77.1 us
    ppermute x0 -> x7, waiting for transfers between devices: none -> 45.9 us  [the longest x4 43.9 us: gather_around(): lower.append(lax.ppermute(lower[-1] if lower else x, axis, pairs))]
    all_gather x1 -> x0, waiting for transfers between devices: 38.8 us -> none  [body(): lax.all_gather(out_weight[0], 'rep', axis=0, tiled=True)]
    all_gather x1, waiting for transfers between devices: 37.8 us -> 0.02 us  [body(): lax.all_gather(in_weight[0], 'rep', axis=0, tiled=True)]
    psum x1, blocking collectives: 27.8 us -> 41.5 us  [body(): grad_gain = lax.psum(gain_total * grad_scale, 'rep')[None]]
    ppermute x0 -> x7, starting transfers between devices: none -> 11.5 us  [the longest x3 10.9 us: gather_around(): upper.append(lax.ppermute(upper[-1] if upper else x, axis, back))]
    unnamed x10 -> x21, local copies, waits for them, and re-layouts: 2.49 us -> 8.02 us
  transfers between devices with their start and end apart: 21 -> 27, of which waited for: 21 -> 25; matrix products, arithmetic and copies ran while one was open for 1% -> 2% of each run, Pallas kernels for 0% -> 0%
where the time goes in v1:
time: 552 us; the launch traced here: 550 us
  waiting for transfers between devices  261 us (47%)
  starting transfers between devices  77.1 us (14%)
  matrix products  68.2 us (12%)
  other arithmetic  53.7 us (10%)
  blocking collectives  41.5 us (8%)
  local copies, waits for them, and re-layouts  33.9 us (6%)
  between operations  14.1 us (3%)
    ppermute x18, waiting for transfers between devices, from_behind(): return lax.ppermute(block, axis, route)  173 us
    ppermute x18, starting transfers between devices, from_behind(): return lax.ppermute(block, axis, route)  65.5 us
    ppermute x4, waiting for transfers between devices, gather_around(): lower.append(lax.ppermute(lower[-1] if lower else x, axis, pairs))  43.9 us
    psum x1, blocking collectives, body(): grad_gain = lax.psum(gain_total * grad_scale, 'rep')[None]  41.5 us
    reduce_scatter x1, waiting for transfers between devices, body(): lax.psum_scatter((jnp.concatenate((left_term, right_term), axis=1) * grad...  41.1 us
    dynamic_update_slice x18, other arithmetic, write_slot(): lax.dynamic_update_index_in_dim(holder, content, slot, 0)  36.3 us
    dot_general x6, matrix products, section_forward(): lax.dot_general(activated, out_weight, (((1,), (1,)), ((), ())), preferre...  29.8 us
    dot_general x6, matrix products, section_forward(): before = jnp.dot(normed, in_weight, preferred_element_type=jnp.float32)  14 us
  transfers between devices with their start and end apart: 27, of which 25 were waited for; matrix products, arithmetic and copies ran while one was open for 2% of the time, Pallas kernels for 0%

profile of v1, /device:TPU:0, one launch (start us, length us, event | category | flops | bytes accessed | tf_op | source)
XLA Modules:
  0.0 550.3 jit_solution(1636127652764327891)
XLA Ops:
  8.5 9.7 %collective-permute-done.2 = bf16[768,256]{1,0:T(8,128)(2,1)S(1)} collective-permute-done((bf16[768,256]{1,0:T(8,128)(2,1)}, bf16[768,256]{1,0:T(8,128)(2,1)S(1)}, u32[]{:S(2)}, u32[]{:S(2)}) %collective-permute-start.2) | collective-permute-done | bytes 393248 | tf_op jit(solution)/shard_map/ppermute | solution.py:23
  21.7 14.7 %collective-permute-done.3 = bf16[768,256]{1,0:T(8,128)(2,1)S(1)} collective-permute-done((bf16[768,256]{1,0:T(8,128)(2,1)S(1)}, bf16[768,256]{1,0:T(8,128)(2,1)S(1)}, u32[]{:S(2)}, u32[]{:S(2)}) %collective-permute-start.3) | collective-permute-done | bytes 393248 | tf_op jit(solution)/shard_map/ppermute | solution.py:23
  42.6 13.3 %collective-permute-done.4 = bf16[768,256]{1,0:T(8,128)(2,1)S(1)} collective-permute-done((bf16[768,256]{1,0:T(8,128)(2,1)S(1)}, bf16[768,256]{1,0:T(8,128)(2,1)S(1)}, u32[]{:S(2)}, u32[]{:S(2)}) %collective-permute-start.4) | collective-permute-done | bytes 393248 | tf_op jit(solution)/shard_map/ppermute | solution.py:23
  63.3 6.2 %collective-permute-done.5 = bf16[768,256]{1,0:T(8,128)(2,1)S(1)} collective-permute-done((bf16[768,256]{1,0:T(8,128)(2,1)S(1)}, bf16[768,256]{1,0:T(8,128)(2,1)S(1)}, u32[]{:S(2)}, u32[]{:S(2)}) %collective-permute-start.5) | collective-permute-done | bytes 393248 | tf_op jit(solution)/shard_map/ppermute | solution.py:23
  80.8 159.6 %while.46 = (s32[]{:T(128)}, bf16[32,6144]{1,0:T(8,128)(2,1)}, bf16[6,32,6144]{2,1,0:T(8,128)(2,1)}, s32[]{:T(128)}, pred[]{:T(512)}, /*index=5*/bf16[6,32,6144]...) while((s32[]{:T(128)}, bf16[32,6144]{1,0:T(8,128)(2,1)}, ...), condition=%wide.region_4.5_spmd, body=%wide.region_0.4_spmd.sunk | while | flops 203530272 | bytes 12215627 | solution.py:121
  80.8 7.0 %conditional.4 = (bf16[32,6144]{1,0:T(8,128)(2,1)}, bf16[6,32,6144]{2,1,0:T(8,128)(2,1)}) conditional(s32[]{:T(128)} %convert_element_type.183, bf16[6,32,6144]{2,1,0:T(8,128)(2,1)} %get-tuple-element.1063, (pred[]{:T(512)}, s32[]{:T(128)}, bf16[6,32,6144]{2,1,0:T(8,128)(2,1)}, bf16[32,6144]{1,0:T(8,128)(2,1)}, f32[1,6144]{1,0:T(1,128)}, ...), branch_computations={%region_1.1_spmd, %region_2.3_spmd} | conditional | flops 203530272 | bytes 9069612 | solution.py:117
  82.8 5.0 fusion
  89.1 7.6 %collective-permute-done = bf16[32,6144]{1,0:T(8,128)(2,1)S(1)} collective-permute-done((bf16[32,6144]{1,0:T(8,128)(2,1)}, bf16[32,6144]{1,0:T(8,128)(2,1)S(1)}, u32[]{:S(2)}, u32[]{:S(2)}) %collective-permute-start) | collective-permute-done | bytes 393248 | tf_op jit(solution)/shard_map/while/body/eval_jaxpr/ppermute | solution.py:35
  97.5 7.0 %conditional.4 = (bf16[32,6144]{1,0:T(8,128)(2,1)}, bf16[6,32,6144]{2,1,0:T(8,128)(2,1)}) conditional(s32[]{:T(128)} %convert_element_type.183, bf16[6,32,6144]{2,1,0:T(8,128)(2,1)} %get-tuple-element.1063, (pred[]{:T(512)}, s32[]{:T(128)}, bf16[6,32,6144]{2,1,0:T(8,128)(2,1)}, bf16[32,6144]{1,0:T(8,128)(2,1)}, f32[1,6144]{1,0:T(1,128)}, ...), branch_computations={%region_1.1_spmd, %region_2.3_spmd} | conditional | flops 203530272 | bytes 9069612 | solution.py:117
  99.5 5.0 fusion
  108.9 6.7 %collective-permute-done = bf16[32,6144]{1,0:T(8,128)(2,1)S(1)} collective-permute-done((bf16[32,6144]{1,0:T(8,128)(2,1)}, bf16[32,6144]{1,0:T(8,128)(2,1)S(1)}, u32[]{:S(2)}, u32[]{:S(2)}) %collective-permute-start) | collective-permute-done | bytes 393248 | tf_op jit(solution)/shard_map/while/body/eval_jaxpr/ppermute | solution.py:35
  116.4 7.0 %conditional.4 = (bf16[32,6144]{1,0:T(8,128)(2,1)}, bf16[6,32,6144]{2,1,0:T(8,128)(2,1)}) conditional(s32[]{:T(128)} %convert_element_type.183, bf16[6,32,6144]{2,1,0:T(8,128)(2,1)} %get-tuple-element.1063, (pred[]{:T(512)}, s32[]{:T(128)}, bf16[6,32,6144]{2,1,0:T(8,128)(2,1)}, bf16[32,6144]{1,0:T(8,128)(2,1)}, f32[1,6144]{1,0:T(1,128)}, ...), branch_computations={%region_1.1_spmd, %region_2.3_spmd} | conditional | flops 203530272 | bytes 9069612 | solution.py:117
  118.4 5.0 fusion
  127.8 5.9 %collective-permute-done = bf16[32,6144]{1,0:T(8,128)(2,1)S(1)} collective-permute-done((bf16[32,6144]{1,0:T(8,128)(2,1)}, bf16[32,6144]{1,0:T(8,128)(2,1)S(1)}, u32[]{:S(2)}, u32[]{:S(2)}) %collective-permute-start) | collective-permute-done | bytes 393248 | tf_op jit(solution)/shard_map/while/body/eval_jaxpr/ppermute | solution.py:35
  134.4 7.0 %conditional.4 = (bf16[32,6144]{1,0:T(8,128)(2,1)}, bf16[6,32,6144]{2,1,0:T(8,128)(2,1)}) conditional(s32[]{:T(128)} %convert_element_type.183, bf16[6,32,6144]{2,1,0:T(8,128)(2,1)} %get-tuple-element.1063, (pred[]{:T(512)}, s32[]{:T(128)}, bf16[6,32,6144]{2,1,0:T(8,128)(2,1)}, bf16[32,6144]{1,0:T(8,128)(2,1)}, f32[1,6144]{1,0:T(1,128)}, ...), branch_computations={%region_1.1_spmd, %region_2.3_spmd} | conditional | flops 203530272 | bytes 9069612 | solution.py:117
  136.5 5.0 fusion
  145.9 5.6 %collective-permute-done = bf16[32,6144]{1,0:T(8,128)(2,1)S(1)} collective-permute-done((bf16[32,6144]{1,0:T(8,128)(2,1)}, bf16[32,6144]{1,0:T(8,128)(2,1)S(1)}, u32[]{:S(2)}, u32[]{:S(2)}) %collective-permute-start) | collective-permute-done | bytes 393248 | tf_op jit(solution)/shard_map/while/body/eval_jaxpr/ppermute | solution.py:35
  152.2 7.0 %conditional.4 = (bf16[32,6144]{1,0:T(8,128)(2,1)}, bf16[6,32,6144]{2,1,0:T(8,128)(2,1)}) conditional(s32[]{:T(128)} %convert_element_type.183, bf16[6,32,6144]{2,1,0:T(8,128)(2,1)} %get-tuple-element.1063, (pred[]{:T(512)}, s32[]{:T(128)}, bf16[6,32,6144]{2,1,0:T(8,128)(2,1)}, bf16[32,6144]{1,0:T(8,128)(2,1)}, f32[1,6144]{1,0:T(1,128)}, ...), branch_computations={%region_1.1_spmd, %region_2.3_spmd} | conditional | flops 203530272 | bytes 9069612 | solution.py:117
  154.3 5.0 fusion
  163.7 5.6 %collective-permute-done = bf16[32,6144]{1,0:T(8,128)(2,1)S(1)} collective-permute-done((bf16[32,6144]{1,0:T(8,128)(2,1)}, bf16[32,6144]{1,0:T(8,128)(2,1)S(1)}, u32[]{:S(2)}, u32[]{:S(2)}) %collective-permute-start) | collective-permute-done | bytes 393248 | tf_op jit(solution)/shard_map/while/body/eval_jaxpr/ppermute | solution.py:35
  170.0 7.0 %conditional.4 = (bf16[32,6144]{1,0:T(8,128)(2,1)}, bf16[6,32,6144]{2,1,0:T(8,128)(2,1)}) conditional(s32[]{:T(128)} %convert_element_type.183, bf16[6,32,6144]{2,1,0:T(8,128)(2,1)} %get-tuple-element.1063, (pred[]{:T(512)}, s32[]{:T(128)}, bf16[6,32,6144]{2,1,0:T(8,128)(2,1)}, bf16[32,6144]{1,0:T(8,128)(2,1)}, f32[1,6144]{1,0:T(1,128)}, ...), branch_computations={%region_1.1_spmd, %region_2.3_spmd} | conditional | flops 203530272 | bytes 9069612 | solution.py:117
  172.0 5.0 fusion
  177.0 5.3 collective-permute-start
  182.3 5.6 %collective-permute-done = bf16[32,6144]{1,0:T(8,128)(2,1)S(1)} collective-permute-done((bf16[32,6144]{1,0:T(8,128)(2,1)}, bf16[32,6144]{1,0:T(8,128)(2,1)S(1)}, u32[]{:S(2)}, u32[]{:S(2)}) %collective-permute-start) | collective-permute-done | bytes 393248 | tf_op jit(solution)/shard_map/while/body/eval_jaxpr/ppermute | solution.py:35
  189.4 11.6 %collective-permute-start = (bf16[32,6144]{1,0:T(8,128)(2,1)}, bf16[32,6144]{1,0:T(8,128)(2,1)S(1)}, u32[]{:S(2)}, u32[]{:S(2)}) collective-permute-start(bf16[32,6144]{1,0:T(8,128)(2,1)} %get-tuple-element.1007), channel_id=1, source_target_pairs={{0,8},{8,16},{16,24},{1,9},{9,17},{17,25},{2,10},{10,18},{18,26},{... | collective-permute-start | bytes 1179656 | tf_op jit(solution)/shard_map/while/body/eval_jaxpr/ppermute | solution.py:35
  201.0 6.3 %collective-permute-done = bf16[32,6144]{1,0:T(8,128)(2,1)S(1)} collective-permute-done((bf16[32,6144]{1,0:T(8,128)(2,1)}, bf16[32,6144]{1,0:T(8,128)(2,1)S(1)}, u32[]{:S(2)}, u32[]{:S(2)}) %collective-permute-start) | collective-permute-done | bytes 393248 | tf_op jit(solution)/shard_map/while/body/eval_jaxpr/ppermute | solution.py:35
  208.7 4.5 collective-permute-start
  213.3 5.6 %collective-permute-done = bf16[32,6144]{1,0:T(8,128)(2,1)S(1)} collective-permute-done((bf16[32,6144]{1,0:T(8,128)(2,1)}, bf16[32,6144]{1,0:T(8,128)(2,1)S(1)}, u32[]{:S(2)}, u32[]{:S(2)}) %collective-permute-start) | collective-permute-done | bytes 393248 | tf_op jit(solution)/shard_map/while/body/eval_jaxpr/ppermute | solution.py:35
  220.3 13.7 %collective-permute-start = (bf16[32,6144]{1,0:T(8,128)(2,1)}, bf16[32,6144]{1,0:T(8,128)(2,1)S(1)}, u32[]{:S(2)}, u32[]{:S(2)}) collective-permute-start(bf16[32,6144]{1,0:T(8,128)(2,1)} %get-tuple-element.1007), channel_id=1, source_target_pairs={{0,8},{8,16},{16,24},{1,9},{9,17},{17,25},{2,10},{10,18},{18,26},{... | collective-permute-start | bytes 1179656 | tf_op jit(solution)/shard_map/while/body/eval_jaxpr/ppermute | solution.py:35
  234.1 5.6 %collective-permute-done = bf16[32,6144]{1,0:T(8,128)(2,1)S(1)} collective-permute-done((bf16[32,6144]{1,0:T(8,128)(2,1)}, bf16[32,6144]{1,0:T(8,128)(2,1)S(1)}, u32[]{:S(2)}, u32[]{:S(2)}) %collective-permute-start) | collective-permute-done | bytes 393248 | tf_op jit(solution)/shard_map/while/body/eval_jaxpr/ppermute | solution.py:35
  247.9 201.3 %while.47 = (s32[]{:T(128)}, bf16[32,6144]{1,0:T(8,128)(2,1)S(1)}, bf16[6,32,6144]{2,1,0:T(8,128)(2,1)}, bf16[6,32,256]{2,1,0:T(8,128)(2,1)}, bf16[6,32,6144]{2,...) while((s32[]{:T(128)}, bf16[32,6144]{1,0:T(8,128)(2,1)S(1)}, ...), condition=%wide.region_11.12_spmd, body=%wide.region_5.11_spmd.sunk | while | flops 307413088 | bytes 30807244 | solution.py:156
  250.0 13.5 %collective-permute-done.1 = bf16[32,6144]{1,0:T(8,128)(2,1)S(1)} collective-permute-done((bf16[32,6144]{1,0:T(8,128)(2,1)}, bf16[32,6144]{1,0:T(8,128)(2,1)S(1)}, u32[]{:S(2)}, u32[]{:S(2)}) %collective-permute-start.1) | collective-permute-done | bytes 393248 | tf_op jit(solution)/shard_map/while/body/eval_jaxpr/ppermute | solution.py:35
  265.5 8.6 %collective-permute-done.1 = bf16[32,6144]{1,0:T(8,128)(2,1)S(1)} collective-permute-done((bf16[32,6144]{1,0:T(8,128)(2,1)}, bf16[32,6144]{1,0:T(8,128)(2,1)S(1)}, u32[]{:S(2)}, u32[]{:S(2)}) %collective-permute-start.1) | collective-permute-done | bytes 393248 | tf_op jit(solution)/shard_map/while/body/eval_jaxpr/ppermute | solution.py:35
  276.2 37.8 %collective-permute-done.1 = bf16[32,6144]{1,0:T(8,128)(2,1)S(1)} collective-permute-done((bf16[32,6144]{1,0:T(8,128)(2,1)}, bf16[32,6144]{1,0:T(8,128)(2,1)S(1)}, u32[]{:S(2)}, u32[]{:S(2)}) %collective-permute-start.1) | collective-permute-done | bytes 393248 | tf_op jit(solution)/shard_map/while/body/eval_jaxpr/ppermute | solution.py:35
  314.0 11.4 %conditional.5 = (bf16[32,6144]{1,0:T(8,128)(2,1)}, bf16[6,32,6144]{2,1,0:T(8,128)(2,1)}, bf16[6,32,256]{2,1,0:T(8,128)(2,1)}, bf16[6,32,6144]{2,1,0:T(8,128)(2,...) conditional(s32[]{:T(128)} %convert_element_type.184, ...), branch_computations={%region_6.6_spmd, %region_7.10_spmd} | conditional | flops 307413088 | bytes 29233976 | solution.py:150
  326.7 9.4 %collective-permute-done.1 = bf16[32,6144]{1,0:T(8,128)(2,1)S(1)} collective-permute-done((bf16[32,6144]{1,0:T(8,128)(2,1)}, bf16[32,6144]{1,0:T(8,128)(2,1)S(1)}, u32[]{:S(2)}, u32[]{:S(2)}) %collective-permute-start.1) | collective-permute-done | bytes 393248 | tf_op jit(solution)/shard_map/while/body/eval_jaxpr/ppermute | solution.py:35
  336.1 11.3 %conditional.5 = (bf16[32,6144]{1,0:T(8,128)(2,1)}, bf16[6,32,6144]{2,1,0:T(8,128)(2,1)}, bf16[6,32,256]{2,1,0:T(8,128)(2,1)}, bf16[6,32,6144]{2,1,0:T(8,128)(2,...) conditional(s32[]{:T(128)} %convert_element_type.184, ...), branch_computations={%region_6.6_spmd, %region_7.10_spmd} | conditional | flops 307413088 | bytes 29233976 | solution.py:150
  348.7 9.5 %collective-permute-done.1 = bf16[32,6144]{1,0:T(8,128)(2,1)S(1)} collective-permute-done((bf16[32,6144]{1,0:T(8,128)(2,1)}, bf16[32,6144]{1,0:T(8,128)(2,1)S(1)}, u32[]{:S(2)}, u32[]{:S(2)}) %collective-permute-start.1) | collective-permute-done | bytes 393248 | tf_op jit(solution)/shard_map/while/body/eval_jaxpr/ppermute | solution.py:35
  358.2 11.4 %conditional.5 = (bf16[32,6144]{1,0:T(8,128)(2,1)}, bf16[6,32,6144]{2,1,0:T(8,128)(2,1)}, bf16[6,32,256]{2,1,0:T(8,128)(2,1)}, bf16[6,32,6144]{2,1,0:T(8,128)(2,...) conditional(s32[]{:T(128)} %convert_element_type.184, ...), branch_computations={%region_6.6_spmd, %region_7.10_spmd} | conditional | flops 307413088 | bytes 29233976 | solution.py:150
  370.9 9.5 %collective-permute-done.1 = bf16[32,6144]{1,0:T(8,128)(2,1)S(1)} collective-permute-done((bf16[32,6144]{1,0:T(8,128)(2,1)}, bf16[32,6144]{1,0:T(8,128)(2,1)S(1)}, u32[]{:S(2)}, u32[]{:S(2)}) %collective-permute-start.1) | collective-permute-done | bytes 393248 | tf_op jit(solution)/shard_map/while/body/eval_jaxpr/ppermute | solution.py:35
  380.3 11.4 %conditional.5 = (bf16[32,6144]{1,0:T(8,128)(2,1)}, bf16[6,32,6144]{2,1,0:T(8,128)(2,1)}, bf16[6,32,256]{2,1,0:T(8,128)(2,1)}, bf16[6,32,6144]{2,1,0:T(8,128)(2,...) conditional(s32[]{:T(128)} %convert_element_type.184, ...), branch_computations={%region_6.6_spmd, %region_7.10_spmd} | conditional | flops 307413088 | bytes 29233976 | solution.py:150
  393.0 9.9 %collective-permute-done.1 = bf16[32,6144]{1,0:T(8,128)(2,1)S(1)} collective-permute-done((bf16[32,6144]{1,0:T(8,128)(2,1)}, bf16[32,6144]{1,0:T(8,128)(2,1)S(1)}, u32[]{:S(2)}, u32[]{:S(2)}) %collective-permute-start.1) | collective-permute-done | bytes 393248 | tf_op jit(solution)/shard_map/while/body/eval_jaxpr/ppermute | solution.py:35
  402.9 11.4 %conditional.5 = (bf16[32,6144]{1,0:T(8,128)(2,1)}, bf16[6,32,6144]{2,1,0:T(8,128)(2,1)}, bf16[6,32,256]{2,1,0:T(8,128)(2,1)}, bf16[6,32,6144]{2,1,0:T(8,128)(2,...) conditional(s32[]{:T(128)} %convert_element_type.184, ...), branch_computations={%region_6.6_spmd, %region_7.10_spmd} | conditional | flops 307413088 | bytes 29233976 | solution.py:150
  415.5 12.4 %collective-permute-done.1 = bf16[32,6144]{1,0:T(8,128)(2,1)S(1)} collective-permute-done((bf16[32,6144]{1,0:T(8,128)(2,1)}, bf16[32,6144]{1,0:T(8,128)(2,1)S(1)}, u32[]{:S(2)}, u32[]{:S(2)}) %collective-permute-start.1) | collective-permute-done | bytes 393248 | tf_op jit(solution)/shard_map/while/body/eval_jaxpr/ppermute | solution.py:35
  428.0 11.4 %conditional.5 = (bf16[32,6144]{1,0:T(8,128)(2,1)}, bf16[6,32,6144]{2,1,0:T(8,128)(2,1)}, bf16[6,32,256]{2,1,0:T(8,128)(2,1)}, bf16[6,32,6144]{2,1,0:T(8,128)(2,...) conditional(s32[]{:T(128)} %convert_element_type.184, ...), branch_computations={%region_6.6_spmd, %region_7.10_spmd} | conditional | flops 307413088 | bytes 29233976 | solution.py:150
  440.6 8.6 %collective-permute-done.1 = bf16[32,6144]{1,0:T(8,128)(2,1)S(1)} collective-permute-done((bf16[32,6144]{1,0:T(8,128)(2,1)}, bf16[32,6144]{1,0:T(8,128)(2,1)S(1)}, u32[]{:S(2)}, u32[]{:S(2)}) %collective-permute-start.1) | collective-permute-done | bytes 393248 | tf_op jit(solution)/shard_map/while/body/eval_jaxpr/ppermute | solution.py:35
  457.8 41.5 %psum.7 = f32[1,6144]{1,0:T(1,128)} all-reduce(f32[1,6144]{1,0:T(1,128)S(1)} %bitcast.98), channel_id=1, replica_groups=mesh['section'=4,'rep'=8] {'rep'}, use_global_device_ids=true, to_apply=%region_13.14 | all-reduce | flops 6144 | bytes 49152 | tf_op jit(solution)/shard_map/psum | solution.py:180
  499.3 41.1 %reduce-scatter.2.cloned.1.call-done = bf16[768,512]{0,1:T(8,128)(2,1)} async-done(((bf16[6144,512]{0,1:T(8,128)(2,1)}), bf16[768,512]{0,1:T(8,128)(2,1)}) %reduce-scatter.2.cloned.1.call-update) | async-done | bytes 786448 | tf_op jit(solution)/shard_map/reduce_scatter | solution.py:172
  (208 shorter events, 175.5 us)
Async XLA Ops:
  7.2 71.2 %all-gather.3.cloned.1.call-start = ((), (), s32[]{:S(2)}) async-start(), calls=%async_computation.2 | async-start | bytes 3538944 | tf_op jit(solution)/shard_map/all_gather | solution.py:89
  7.9 532.6 %reduce-scatter.2.cloned.1.call-start = ((), (), s32[]{:S(2)}) async-start(), calls=%async_computation.1 | async-start | bytes 7077888 | tf_op jit(solution)/shard_map/reduce_scatter | solution.py:172
  7.9 10.2 %collective-permute-start.2 = (bf16[768,256]{1,0:T(8,128)(2,1)}, bf16[768,256]{1,0:T(8,128)(2,1)S(1)}, u32[]{:S(2)}, u32[]{:S(2)}) collective-permute-start(bf16[768,256]{1,0:T(8,128)(2,1)} %bitcast.96), channel_id=1, source_target_pairs={{0,1},{1,2},{2,3},{3,4},{4,5},{5,6},{6,7},{7,0},{8,9},{9,10},{10,1... | collective-permute-start | bytes 1179656 | tf_op jit(solution)/shard_map/ppermute | solution.py:23
  18.2 18.2 %collective-permute-start.3 = (bf16[768,256]{1,0:T(8,128)(2,1)S(1)}, bf16[768,256]{1,0:T(8,128)(2,1)S(1)}, u32[]{:S(2)}, u32[]{:S(2)}) collective-permute-start(bf16[768,256]{1,0:T(8,128)(2,1)S(1)} %collective-permute-done.2), channel_id=1, source_target_pairs={{0,1},{1,2},{2,3},{3,4},{4,5},{5,6},{6,7},{7,0},{8,9},{9,10},{10,1... | collective-permute-start | bytes 1179656 | tf_op jit(solution)/shard_map/ppermute | solution.py:23
  18.2 20.8 %collective-permute-start.6 = (bf16[768,256]{1,0:T(8,128)(2,1)}, bf16[768,256]{1,0:T(8,128)(2,1)S(1)}, u32[]{:S(2)}, u32[]{:S(2)}) collective-permute-start(bf16[768,256]{1,0:T(8,128)(2,1)} %bitcast.97), channel_id=1, source_target_pairs={{1,0},{2,1},{3,2},{4,3},{5,4},{6,5},{7,6},{0,7},{9,8},{10,9},{11,1... | collective-permute-start | bytes 1179656 | tf_op jit(solution)/shard_map/ppermute | solution.py:25
  36.4 19.6 %collective-permute-start.4 = (bf16[768,256]{1,0:T(8,128)(2,1)S(1)}, bf16[768,256]{1,0:T(8,128)(2,1)S(1)}, u32[]{:S(2)}, u32[]{:S(2)}) collective-permute-start(bf16[768,256]{1,0:T(8,128)(2,1)S(1)} %collective-permute-done.3), channel_id=1, source_target_pairs={{0,1},{1,2},{2,3},{3,4},{4,5},{5,6},{6,7},{7,0},{8,9},{9,10},{10,1... | collective-permute-start | bytes 1179656 | tf_op jit(solution)/shard_map/ppermute | solution.py:23
  37.1 35.4 %copy-start.9 = (bf16[1,768,256]{2,1,0:T(8,128)(2,1)S(1)}, bf16[1,768,256]{2,1,0:T(8,128)(2,1)}, u32[]{:S(2)}) copy-start(bf16[1,768,256]{2,1,0:T(8,128)(2,1)} %param.17) | copy-start | bytes 1179652
  39.0 20.6 %collective-permute-start.7 = (bf16[768,256]{1,0:T(8,128)(2,1)S(1)}, bf16[768,256]{1,0:T(8,128)(2,1)S(1)}, u32[]{:S(2)}, u32[]{:S(2)}) collective-permute-start(bf16[768,256]{1,0:T(8,128)(2,1)S(1)} %collective-permute-done.6), channel_id=1, source_target_pairs={{1,0},{2,1},{3,2},{4,3},{5,4},{6,5},{7,6},{0,7},{9,8},{10,9},{11,1... | collective-permute-start | bytes 1179656 | tf_op jit(solution)/shard_map/ppermute | solution.py:25
  56.0 13.5 %collective-permute-start.5 = (bf16[768,256]{1,0:T(8,128)(2,1)S(1)}, bf16[768,256]{1,0:T(8,128)(2,1)S(1)}, u32[]{:S(2)}, u32[]{:S(2)}) collective-permute-start(bf16[768,256]{1,0:T(8,128)(2,1)S(1)} %collective-permute-done.4), channel_id=1, source_target_pairs={{0,1},{1,2},{2,3},{3,4},{4,5},{5,6},{6,7},{7,0},{8,9},{9,10},{10,1... | collective-permute-start | bytes 1179656 | tf_op jit(solution)/shard_map/ppermute | solution.py:23
  59.6 15.3 %collective-permute-start.8 = (bf16[768,256]{1,0:T(8,128)(2,1)S(1)}, bf16[768,256]{1,0:T(8,128)(2,1)S(1)}, u32[]{:S(2)}, u32[]{:S(2)}) collective-permute-start(bf16[768,256]{1,0:T(8,128)(2,1)S(1)} %collective-permute-done.7), channel_id=1, source_target_pairs={{1,0},{2,1},{3,2},{4,3},{5,4},{6,5},{7,6},{0,7},{9,8},{10,9},{11,1... | collective-permute-start | bytes 1179656 | tf_op jit(solution)/shard_map/ppermute | solution.py:25
  87.8 8.9 %collective-permute-start = (bf16[32,6144]{1,0:T(8,128)(2,1)}, bf16[32,6144]{1,0:T(8,128)(2,1)S(1)}, u32[]{:S(2)}, u32[]{:S(2)}) collective-permute-start(bf16[32,6144]{1,0:T(8,128)(2,1)} %get-tuple-element.1007), channel_id=1, source_target_pairs={{0,8},{8,16},{16,24},{1,9},{9,17},{17,25},{2,10},{10,18},{18,26},{... | collective-permute-start | bytes 1179656 | tf_op jit(solution)/shard_map/while/body/eval_jaxpr/ppermute | solution.py:35
  104.5 11.2 %collective-permute-start = (bf16[32,6144]{1,0:T(8,128)(2,1)}, bf16[32,6144]{1,0:T(8,128)(2,1)S(1)}, u32[]{:S(2)}, u32[]{:S(2)}) collective-permute-start(bf16[32,6144]{1,0:T(8,128)(2,1)} %get-tuple-element.1007), channel_id=1, source_target_pairs={{0,8},{8,16},{16,24},{1,9},{9,17},{17,25},{2,10},{10,18},{18,26},{... | collective-permute-start | bytes 1179656 | tf_op jit(solution)/shard_map/while/body/eval_jaxpr/ppermute | solution.py:35
  123.4 10.3 %collective-permute-start = (bf16[32,6144]{1,0:T(8,128)(2,1)}, bf16[32,6144]{1,0:T(8,128)(2,1)S(1)}, u32[]{:S(2)}, u32[]{:S(2)}) collective-permute-start(bf16[32,6144]{1,0:T(8,128)(2,1)} %get-tuple-element.1007), channel_id=1, source_target_pairs={{0,8},{8,16},{16,24},{1,9},{9,17},{17,25},{2,10},{10,18},{18,26},{... | collective-permute-start | bytes 1179656 | tf_op jit(solution)/shard_map/while/body/eval_jaxpr/ppermute | solution.py:35
  141.5 10.0 %collective-permute-start = (bf16[32,6144]{1,0:T(8,128)(2,1)}, bf16[32,6144]{1,0:T(8,128)(2,1)S(1)}, u32[]{:S(2)}, u32[]{:S(2)}) collective-permute-start(bf16[32,6144]{1,0:T(8,128)(2,1)} %get-tuple-element.1007), channel_id=1, source_target_pairs={{0,8},{8,16},{16,24},{1,9},{9,17},{17,25},{2,10},{10,18},{18,26},{... | collective-permute-start | bytes 1179656 | tf_op jit(solution)/shard_map/while/body/eval_jaxpr/ppermute | solution.py:35
  159.2 10.0 %collective-permute-start = (bf16[32,6144]{1,0:T(8,128)(2,1)}, bf16[32,6144]{1,0:T(8,128)(2,1)S(1)}, u32[]{:S(2)}, u32[]{:S(2)}) collective-permute-start(bf16[32,6144]{1,0:T(8,128)(2,1)} %get-tuple-element.1007), channel_id=1, source_target_pairs={{0,8},{8,16},{16,24},{1,9},{9,17},{17,25},{2,10},{10,18},{18,26},{... | collective-permute-start | bytes 1179656 | tf_op jit(solution)/shard_map/while/body/eval_jaxpr/ppermute | solution.py:35
  177.0 10.9 %collective-permute-start = (bf16[32,6144]{1,0:T(8,128)(2,1)}, bf16[32,6144]{1,0:T(8,128)(2,1)S(1)}, u32[]{:S(2)}, u32[]{:S(2)}) collective-permute-start(bf16[32,6144]{1,0:T(8,128)(2,1)} %get-tuple-element.1007), channel_id=1, source_target_pairs={{0,8},{8,16},{16,24},{1,9},{9,17},{17,25},{2,10},{10,18},{18,26},{... | collective-permute-start | bytes 1179656 | tf_op jit(solution)/shard_map/while/body/eval_jaxpr/ppermute | solution.py:35
  189.4 17.8 %collective-permute-start = (bf16[32,6144]{1,0:T(8,128)(2,1)}, bf16[32,6144]{1,0:T(8,128)(2,1)S(1)}, u32[]{:S(2)}, u32[]{:S(2)}) collective-permute-start(bf16[32,6144]{1,0:T(8,128)(2,1)} %get-tuple-element.1007), channel_id=1, source_target_pairs={{0,8},{8,16},{16,24},{1,9},{9,17},{17,25},{2,10},{10,18},{18,26},{... | collective-permute-start | bytes 1179656 | tf_op jit(solution)/shard_map/while/body/eval_jaxpr/ppermute | solution.py:35
  208.7 10.1 %collective-permute-start = (bf16[32,6144]{1,0:T(8,128)(2,1)}, bf16[32,6144]{1,0:T(8,128)(2,1)S(1)}, u32[]{:S(2)}, u32[]{:S(2)}) collective-permute-start(bf16[32,6144]{1,0:T(8,128)(2,1)} %get-tuple-element.1007), channel_id=1, source_target_pairs={{0,8},{8,16},{16,24},{1,9},{9,17},{17,25},{2,10},{10,18},{18,26},{... | collective-permute-start | bytes 1179656 | tf_op jit(solution)/shard_map/while/body/eval_jaxpr/ppermute | solution.py:35
  220.3 19.3 %collective-permute-start = (bf16[32,6144]{1,0:T(8,128)(2,1)}, bf16[32,6144]{1,0:T(8,128)(2,1)S(1)}, u32[]{:S(2)}, u32[]{:S(2)}) collective-permute-start(bf16[32,6144]{1,0:T(8,128)(2,1)} %get-tuple-element.1007), channel_id=1, source_target_pairs={{0,8},{8,16},{16,24},{1,9},{9,17},{17,25},{2,10},{10,18},{18,26},{... | collective-permute-start | bytes 1179656 | tf_op jit(solution)/shard_map/while/body/eval_jaxpr/ppermute | solution.py:35
  242.8 5.2 copy-start
  248.7 14.8 %collective-permute-start.1 = (bf16[32,6144]{1,0:T(8,128)(2,1)}, bf16[32,6144]{1,0:T(8,128)(2,1)S(1)}, u32[]{:S(2)}, u32[]{:S(2)}) collective-permute-start(bf16[32,6144]{1,0:T(8,128)(2,1)} %get-tuple-element.1024), channel_id=1, source_target_pairs={{8,0},{16,8},{24,16},{9,1},{17,9},{25,17},{10,2},{18,10},{26,18},{... | collective-permute-start | bytes 1179656 | tf_op jit(solution)/shard_map/while/body/eval_jaxpr/ppermute | solution.py:35
  264.2 9.9 %collective-permute-start.1 = (bf16[32,6144]{1,0:T(8,128)(2,1)}, bf16[32,6144]{1,0:T(8,128)(2,1)S(1)}, u32[]{:S(2)}, u32[]{:S(2)}) collective-permute-start(bf16[32,6144]{1,0:T(8,128)(2,1)} %get-tuple-element.1024), channel_id=1, source_target_pairs={{8,0},{16,8},{24,16},{9,1},{17,9},{25,17},{10,2},{18,10},{26,18},{... | collective-permute-start | bytes 1179656 | tf_op jit(solution)/shard_map/while/body/eval_jaxpr/ppermute | solution.py:35
  274.9 39.1 %collective-permute-start.1 = (bf16[32,6144]{1,0:T(8,128)(2,1)}, bf16[32,6144]{1,0:T(8,128)(2,1)S(1)}, u32[]{:S(2)}, u32[]{:S(2)}) collective-permute-start(bf16[32,6144]{1,0:T(8,128)(2,1)} %get-tuple-element.1024), channel_id=1, source_target_pairs={{8,0},{16,8},{24,16},{9,1},{17,9},{25,17},{10,2},{18,10},{26,18},{... | collective-permute-start | bytes 1179656 | tf_op jit(solution)/shard_map/while/body/eval_jaxpr/ppermute | solution.py:35
  314.0 5.6 %copy-start.2 = (bf16[6144,256]{1,0:T(8,128)(2,1)S(1)}, bf16[6144,256]{1,0:T(8,128)(2,1)}, u32[]{:S(2)}) copy-start(bf16[6144,256]{1,0:T(8,128)(2,1)} %get-tuple-element.747) | copy-start | bytes 9437188 | tf_op jit(solution)/shard_map/while/body/eval_jaxpr/cond
  319.6 3.4 copy-start.5
  323.0 2.4 copy-start.6
  325.4 10.7 %collective-permute-start.1 = (bf16[32,6144]{1,0:T(8,128)(2,1)}, bf16[32,6144]{1,0:T(8,128)(2,1)S(1)}, u32[]{:S(2)}, u32[]{:S(2)}) collective-permute-start(bf16[32,6144]{1,0:T(8,128)(2,1)} %get-tuple-element.1024), channel_id=1, source_target_pairs={{8,0},{16,8},{24,16},{9,1},{17,9},{25,17},{10,2},{18,10},{26,18},{... | collective-permute-start | bytes 1179656 | tf_op jit(solution)/shard_map/while/body/eval_jaxpr/ppermute | solution.py:35
  336.1 5.5 %copy-start.2 = (bf16[6144,256]{1,0:T(8,128)(2,1)S(1)}, bf16[6144,256]{1,0:T(8,128)(2,1)}, u32[]{:S(2)}) copy-start(bf16[6144,256]{1,0:T(8,128)(2,1)} %get-tuple-element.747) | copy-start | bytes 9437188 | tf_op jit(solution)/shard_map/while/body/eval_jaxpr/cond
  341.6 3.4 copy-start.5
  347.4 10.8 %collective-permute-start.1 = (bf16[32,6144]{1,0:T(8,128)(2,1)}, bf16[32,6144]{1,0:T(8,128)(2,1)S(1)}, u32[]{:S(2)}, u32[]{:S(2)}) collective-permute-start(bf16[32,6144]{1,0:T(8,128)(2,1)} %get-tuple-element.1024), channel_id=1, source_target_pairs={{8,0},{16,8},{24,16},{9,1},{17,9},{25,17},{10,2},{18,10},{26,18},{... | collective-permute-start | bytes 1179656 | tf_op jit(solution)/shard_map/while/body/eval_jaxpr/ppermute | solution.py:35
  358.2 5.5 %copy-start.2 = (bf16[6144,256]{1,0:T(8,128)(2,1)S(1)}, bf16[6144,256]{1,0:T(8,128)(2,1)}, u32[]{:S(2)}) copy-start(bf16[6144,256]{1,0:T(8,128)(2,1)} %get-tuple-element.747) | copy-start | bytes 9437188 | tf_op jit(solution)/shard_map/while/body/eval_jaxpr/cond
  363.7 3.4 copy-start.5
  367.2 2.4 copy-start.6
  369.6 10.8 %collective-permute-start.1 = (bf16[32,6144]{1,0:T(8,128)(2,1)}, bf16[32,6144]{1,0:T(8,128)(2,1)S(1)}, u32[]{:S(2)}, u32[]{:S(2)}) collective-permute-start(bf16[32,6144]{1,0:T(8,128)(2,1)} %get-tuple-element.1024), channel_id=1, source_target_pairs={{8,0},{16,8},{24,16},{9,1},{17,9},{25,17},{10,2},{18,10},{26,18},{... | collective-permute-start | bytes 1179656 | tf_op jit(solution)/shard_map/while/body/eval_jaxpr/ppermute | solution.py:35
  380.3 5.5 %copy-start.2 = (bf16[6144,256]{1,0:T(8,128)(2,1)S(1)}, bf16[6144,256]{1,0:T(8,128)(2,1)}, u32[]{:S(2)}) copy-start(bf16[6144,256]{1,0:T(8,128)(2,1)} %get-tuple-element.747) | copy-start | bytes 9437188 | tf_op jit(solution)/shard_map/while/body/eval_jaxpr/cond
  385.8 3.4 copy-start.5
  389.3 2.4 copy-start.6
  391.7 11.2 %collective-permute-start.1 = (bf16[32,6144]{1,0:T(8,128)(2,1)}, bf16[32,6144]{1,0:T(8,128)(2,1)S(1)}, u32[]{:S(2)}, u32[]{:S(2)}) collective-permute-start(bf16[32,6144]{1,0:T(8,128)(2,1)} %get-tuple-element.1024), channel_id=1, source_target_pairs={{8,0},{16,8},{24,16},{9,1},{17,9},{25,17},{10,2},{18,10},{26,18},{... | collective-permute-start | bytes 1179656 | tf_op jit(solution)/shard_map/while/body/eval_jaxpr/ppermute | solution.py:35
  402.9 5.5 %copy-start.2 = (bf16[6144,256]{1,0:T(8,128)(2,1)S(1)}, bf16[6144,256]{1,0:T(8,128)(2,1)}, u32[]{:S(2)}) copy-start(bf16[6144,256]{1,0:T(8,128)(2,1)} %get-tuple-element.747) | copy-start | bytes 9437188 | tf_op jit(solution)/shard_map/while/body/eval_jaxpr/cond
  408.4 3.4 copy-start.5
  411.9 2.4 copy-start.6
  414.3 13.7 %collective-permute-start.1 = (bf16[32,6144]{1,0:T(8,128)(2,1)}, bf16[32,6144]{1,0:T(8,128)(2,1)S(1)}, u32[]{:S(2)}, u32[]{:S(2)}) collective-permute-start(bf16[32,6144]{1,0:T(8,128)(2,1)} %get-tuple-element.1024), channel_id=1, source_target_pairs={{8,0},{16,8},{24,16},{9,1},{17,9},{25,17},{10,2},{18,10},{26,18},{... | collective-permute-start | bytes 1179656 | tf_op jit(solution)/shard_map/while/body/eval_jaxpr/ppermute | solution.py:35
  428.0 5.5 %copy-start.2 = (bf16[6144,256]{1,0:T(8,128)(2,1)S(1)}, bf16[6144,256]{1,0:T(8,128)(2,1)}, u32[]{:S(2)}) copy-start(bf16[6144,256]{1,0:T(8,128)(2,1)} %get-tuple-element.747) | copy-start | bytes 9437188 | tf_op jit(solution)/shard_map/while/body/eval_jaxpr/cond
  433.5 3.4 copy-start.5
  437.0 2.4 copy-start.6
  439.3 9.9 %collective-permute-start.1 = (bf16[32,6144]{1,0:T(8,128)(2,1)}, bf16[32,6144]{1,0:T(8,128)(2,1)S(1)}, u32[]{:S(2)}, u32[]{:S(2)}) collective-permute-start(bf16[32,6144]{1,0:T(8,128)(2,1)} %get-tuple-element.1024), channel_id=1, source_target_pairs={{8,0},{16,8},{24,16},{9,1},{17,9},{25,17},{10,2},{18,10},{26,18},{... | collective-permute-start | bytes 1179656 | tf_op jit(solution)/shard_map/while/body/eval_jaxpr/ppermute | solution.py:35
  449.2 2.9 copy-start.4
  449.2 2.9 copy-start.8
  (12 other events, 12.2 us)
Sparse Core Ops, SparseCore 0:
  9.6 55.5 all-gather.2
  457.2 83.2 reduce-scatter.1
